TPU v7x, 512 devices: a whole 4x4x16 slice. The times are simulated.
512 devices in a mesh: tile: 32 (over y, x, core), fsdp: 16 (over z).
Axes of the slice: x: 4, y: 4, z: 16, core: 2. Of those that a mesh axis runs over, the one named last changes fastest.
Arguments:
- images: bfloat16 [16, 32, 8, 128, 320], P('fsdp', 'tile'), may hold values from -80 to 80
- tile_rows: int32 [16, 32], P('fsdp', 'tile'), may hold values from 1 to 8, 160 in all within a row
- cotangent: bfloat16 [16, 32, 8, 128, 320], P('fsdp', 'tile'), may hold values from -6 to 6
- master_weight: float32 [2880, 320], P('fsdp'), may hold values from -0.109375 to 0.109375
- norm_gain: float32 [320], replicated, may hold values from 0.5 to 1.5
- norm_bias: float32 [320], replicated, may hold values from -3 to 3
- first_moment: float32 [2880, 320], P('fsdp'), may hold values from -6 to 6
- second_moment: float32 [2880, 320], P('fsdp'), may hold values from 0.5 to 4
Outputs:
- activation: bfloat16 [16, 32, 8, 128, 320], P('fsdp', 'tile')
- image_grad: bfloat16 [16, 32, 8, 128, 320], P('fsdp', 'tile')
- weight_grad: float32 [2880, 320], P('fsdp')
- new_weight: float32 [2880, 320], P('fsdp')
- new_first: float32 [2880, 320], P('fsdp')
- new_second: float32 [2880, 320], P('fsdp')
- gain_grad: float32 [320], replicated
- bias_grad: float32 [320], replicated
Inputs may be any that keep to these rules, and one draw needn't show every extreme that they name: `tile_rows`: in each frame the 32 counts sum to 160 and the largest is exactly 8.
All inputs are finite; a program needn't handle non-finite values. No bound on the sum of `tile_rows` on one device may be relied on, other than what follows from the above.
Results may differ from a plain program's by a relative error of at most 0.027.
Values may be sent and summed in bfloat16 or wider, within the bound.
No kernel may reach another device: no remote copies, remote signals or barrier semaphores. Data moves between devices by JAX's collectives and lax.ppermute only.
A program may use at most 64 MiB of HBM per device.

v0:
```python
import jax
import jax.numpy as jnp
from jax import lax
from jax.sharding import PartitionSpec as P

GROUPS = 32
ROWS_MEAN = 5


def extended(cells, sides, width):
    for axis, dim in sides:
        count = lax.axis_size(axis)
        ends = count - 1
        head = lax.slice_in_dim(cells, 0, width, axis=dim)
        tail = lax.slice_in_dim(cells, cells.shape[dim] - width, cells.shape[dim], axis=dim)
        cells = jnp.concatenate(
            [
                lax.ppermute(tail, axis, [(i, (i + 1) % count) for i in range(ends)]),
                cells,
                lax.ppermute(head, axis, [((i + 1) % count, i) for i in range(ends)]),
            ],
            axis=dim,
        )
    return cells


def edge_pair(source, live_count):
    first_row = source[0:1]
    last_row = lax.dynamic_slice_in_dim(source, live_count - 1, 1, 0)
    return jnp.concatenate([first_row, last_row], axis=0)


def framed(source, beside_all, live_count):
    slot_count = source.shape[0]
    zero_row = jnp.zeros_like(source[0:1])
    stacked = jnp.concatenate([beside_all[0:1], source, zero_row], axis=0)
    marker = (jnp.arange(slot_count + 2) == live_count + 1)[:, None, None]
    stacked = jnp.where(marker, beside_all[3:4], stacked)
    return jnp.pad(stacked, ((0, 0), (1, 1), (0, 0)))


def patches_of(padded, slot_count, cell_cols):
    pieces = [
        padded[row_step : row_step + slot_count, col_step : col_step + cell_cols, :]
        for row_step in range(3)
        for col_step in range(3)
    ]
    return jnp.concatenate(pieces, axis=-1).reshape(slot_count * cell_cols, -1)


def local(
    images, tile_rows, cotangent, master_weight, norm_gain, norm_bias, first_moment, second_moment
):
    slot_count, cell_cols, channels = (images.shape[2], images.shape[3], images.shape[4])
    per_group = channels // GROUPS
    tile_count = lax.axis_size("tile")
    shards = lax.axis_size("fsdp")
    population = jnp.float32(ROWS_MEAN * tile_count * cell_cols * per_group)
    live_count = tile_rows[0, 0]
    live_rows = jnp.arange(slot_count) < live_count
    cell_mask = jnp.repeat(live_rows, cell_cols).astype(jnp.float32)[:, None]

    def grouped(values):
        return jnp.sum(values.reshape(-1, GROUPS, per_group), axis=(0, 2))

    def spread(stat):
        return jnp.repeat(stat, per_group)

    source = jnp.where(live_rows[:, None, None], images[0, 0], jnp.zeros((), jnp.bfloat16))
    beside_all = extended(edge_pair(source, live_count), (("tile", 0),), 1)
    columns = patches_of(framed(source, beside_all, live_count), slot_count, cell_cols)
    gathered = lax.all_gather(master_weight.astype(jnp.bfloat16), "fsdp", axis=0, tiled=True)
    mixed = jnp.dot(columns, gathered, preferred_element_type=jnp.float32)
    group_mean = lax.psum(grouped(mixed * cell_mask), "tile") / population
    centered = (mixed - spread(group_mean)) * cell_mask
    variance = lax.psum(grouped(centered * centered), "tile") / population
    inverse = lax.rsqrt(variance + 1e-05)
    normed = (mixed - spread(group_mean)) * spread(inverse)
    shifted = normed * norm_gain + norm_bias
    gate_value = jax.nn.sigmoid(shifted)
    activation = (shifted * gate_value * cell_mask).astype(jnp.bfloat16).reshape(images.shape)
    upstream = cotangent[0, 0].reshape(-1, channels).astype(jnp.float32) * cell_mask
    dshift = upstream * gate_value * (1.0 + shifted * (1.0 - gate_value))
    scaled = dshift * norm_gain
    delta_sum, cross_sum = lax.psum((grouped(scaled), grouped(scaled * normed)), "tile")
    gain_total, bias_total = lax.psum(
        (jnp.sum(dshift * normed, axis=0), jnp.sum(dshift, axis=0)), ("tile", "fsdp")
    )
    norm_scale = jnp.float32(shards * ROWS_MEAN * tile_count * cell_cols) ** (-0.5)
    pre_grad = spread(inverse) * (
        scaled - spread(delta_sum / population) - normed * spread(cross_sum / population)
    )
    pre_grad = (pre_grad * cell_mask).astype(jnp.bfloat16)
    grad_field = pre_grad.reshape(slot_count, cell_cols, channels)
    grad_around = extended(edge_pair(grad_field, live_count), (("tile", 0),), 1)
    grad_columns = patches_of(framed(grad_field, grad_around, live_count), slot_count, cell_cols)
    flipped = (
        gathered.reshape(9, channels, channels)[::-1]
        .transpose(0, 2, 1)
        .reshape(9 * channels, channels)
    )
    image_grad = (
        (jnp.dot(grad_columns, flipped, preferred_element_type=jnp.float32) * cell_mask)
        .astype(jnp.bfloat16)
        .reshape(images.shape)
    )
    full_grad = lax.psum(
        lax.dot_general(
            columns, pre_grad, (((0,), (0,)), ((), ())), preferred_element_type=jnp.float32
        ).astype(jnp.bfloat16),
        "tile",
    )
    grad_shard = lax.psum_scatter(full_grad, "fsdp", scatter_dimension=0, tiled=True).astype(
        jnp.float32
    )
    weight_grad = grad_shard * norm_scale
    new_first = 0.9 * first_moment + 0.1 * weight_grad
    new_second = 0.999 * second_moment + 0.001 * weight_grad * weight_grad
    first_fix = new_first / (1.0 - 0.9**10)
    second_fix = new_second / (1.0 - 0.999**10)
    new_weight = master_weight - 0.01 * first_fix / (jnp.sqrt(second_fix) + 1e-08)
    return (
        activation,
        image_grad,
        weight_grad,
        new_weight,
        new_first,
        new_second,
        gain_total * norm_scale,
        bias_total * norm_scale,
    )


def solution(mesh):
    placed = (
        P("fsdp", "tile", None, None, None),
        P("fsdp", "tile"),
        P("fsdp", "tile", None, None, None),
        P("fsdp", None),
        P(),
        P(),
        P("fsdp", None),
        P("fsdp", None),
    )
    return jax.shard_map(
        local,
        mesh=mesh,
        in_specs=placed,
        out_specs=(
            P("fsdp", "tile", None, None, None),
            P("fsdp", "tile", None, None, None),
            P("fsdp", None),
            P("fsdp", None),
            P("fsdp", None),
            P("fsdp", None),
            P(),
            P(),
        ),
        check_vma=False,
    )
```

profile of v0, /device:TPU:1, one launch (start us, length us, event | category | flops | bytes accessed | tf_op | source)
XLA Modules:
  0.0 609.0 jit_solution(12582963821743056391)
XLA Ops:
  7.2 1.7 convert_bitcast_fusion
  9.7 1.2 bitcast_select_fusion
  10.9 8.8 %collective-permute-start = (bf16[1,128,320]{1,2,0:T(8,128)(2,1)S(1)}, bf16[1,128,320]{1,2,0:T(8,128)(2,1)S(1)}, u32[]{:S(2)}, u32[]{:S(2)}) collective-permute-start(bf16[1,128,320]{1,2,0:T(8,128)(2,1)S(1)} %get-tuple-element.46), channel_id=1, source_target_pairs={{16,0},{32,16},{48,32},{64,48},{80,64},{96,80},{112,96},{128,112},... | collective-permute-start | bytes 245768 | tf_op jit(solution)/shard_map/ppermute | solution.py:20
  19.7 1.9 collective-permute-start.1
  21.6 1.5 copy.30
  23.2 1.3 dynamic-slice.4
  25.4 1.1 fusion.5
  26.5 1.0 slice_dynamic-update-slice_fusion.5
  27.5 1.1 fusion.6
  28.6 1.1 fusion.7
  29.7 1.0 slice_dynamic-update-slice_fusion.4
  30.7 1.1 fusion.8
  31.8 1.1 fusion.9
  32.9 1.0 slice_dynamic-update-slice_fusion.3
  33.8 1.1 fusion.10
  34.9 8.4 %copy.29 = bf16[8,128,2880]{2,1,0:T(8,128)(2,1)} copy(bf16[8,128,2880]{1,2,0:T(8,128)(2,1)} %fusion.10) | data formatting | bytes 11796480 | tf_op jit(solution)/shard_map/concatenate | solution.py:48
  43.4 37.7 %all-gather.3.cloned.1.call-done = bf16[16,180,320]{2,1,0:T(8,128)(2,1)} async-done(((bf16[1,180,320]{2,1,0:T(8,128)(2,1)}), bf16[16,180,320]{2,1,0:T(8,128)(2,1)}) %all-gather.3.cloned.1.call-update) | async-done | bytes 1843216 | tf_op jit(solution)/shard_map/all_gather | solution.py:72
  81.1 2.8 reshape.78
  83.8 5.1 multiply_reduce_fusion.3
  89.1 71.5 %psum.49 = f32[32]{0:T(128)S(1)} all-reduce(f32[32]{0:T(128)S(1)} %reduce_sum.67), channel_id=1, replica_groups=mesh['tile'=32,'fsdp'=16] {'tile'}, use_global_device_ids=true, to_apply=%region_2.3 | all-reduce | flops 32 | bytes 256 | tf_op jit(solution)/shard_map/psum | solution.py:74
  161.4 62.7 %psum.50 = f32[32]{0:T(128)S(1)} all-reduce(f32[32]{0:T(128)S(1)} %reduce_sum.73), channel_id=1, replica_groups=mesh['tile'=32,'fsdp'=16] {'tile'}, use_global_device_ids=true, to_apply=%region_5.6 | all-reduce | flops 32 | bytes 256 | tf_op jit(solution)/shard_map/psum | solution.py:76
  224.3 3.5 multiply_reduce_fusion
  228.2 62.9 %all-reduce.5 = (f32[32]{0:T(128)S(1)}, f32[32]{0:T(128)S(1)}) all-reduce(f32[32]{0:T(128)S(1)} %reduce_sum.93, f32[32]{0:T(128)S(1)} %reduce_sum.90), channel_id=1, replica_groups=mesh['tile'=32,'fsdp'=16] {'tile'}, use_global_device_ids=true, to_apply=%region_11.12 | all-reduce | flops 64 | bytes 512 | tf_op jit(solution)/shard_map/psum | solution.py:85
  292.3 7.4 %convolution_convert_fusion = bf16[2880,320]{1,0:T(8,128)(2,1)} fusion(bf16[1024,2880]{1,0:T(8,128)(2,1)} %bitcast.60, bf16[1024,320]{0,1:T(8,128)(2,1)S(1)} %multiply_convert_fusion), kind=kOutput, calls=%fused_computation | convolution fusion | flops 1888358400 | bytes 8396800 | tf_op jit(solution)/shard_map/dot_general | solution.py:108
  300.5 33.6 %fusion = bf16[192,320]{1,0:T(8,128)(2,1)S(1)} fusion(bf16[2880,320]{1,0:T(8,128)(2,1)} %convolution_convert_fusion), kind=kCustom, calls=%all-reduce-scatter | all-reduce-scatter fusion | flops 983041 | bytes 1968128
  334.1 2.7 collective-permute-start.4
  337.5 5.1 collective-permute-start.3
  342.6 5.2 collective-permute-start.2
  347.8 100.6 %all-reduce.4 = (f32[320]{0:T(512)S(1)}, f32[320]{0:T(512)S(1)}) all-reduce(f32[320]{0:T(512)S(1)} %get-tuple-element.32, f32[320]{0:T(512)S(1)} %get-tuple-element.35), channel_id=1, replica_groups=mesh['tile'=32,'fsdp'=16] {'tile','fsdp'}, use_global_device_ids=true, to_apply=%region_15.16 | all-reduce | flops 640 | bytes 5120 | tf_op jit(solution)/shard_map/psum | solution.py:86
  449.0 2.2 reshape.73
  451.2 1.8 reverse_bitcast_fusion
  453.1 2.5 copy.34
  455.6 1.2 copy.38
  456.8 0.9 copy.35
  457.9 1.1 fusion.11
  459.0 1.0 slice_dynamic-update-slice_fusion.2
  460.0 1.1 fusion.12
  461.2 1.1 fusion.13
  462.3 1.0 slice_dynamic-update-slice_fusion.1
  463.3 1.1 fusion.14
  464.3 1.1 fusion.15
  465.4 1.0 slice_dynamic-update-slice_fusion
  466.4 1.1 fusion.16
  467.5 8.6 %copy.33 = bf16[8,128,2880]{2,1,0:T(8,128)(2,1)} copy(bf16[8,128,2880]{1,2,0:T(8,128)(2,1)} %fusion.16) | data formatting | bytes 11796480 | tf_op jit(solution)/shard_map/concatenate | solution.py:48
  477.7 4.9 fusion.4
  482.8 0.9 copy.36
  483.8 116.3 %all-reduce.8.cloned.1.call-done = bf16[180,320]{1,0:T(8,128)(2,1)} async-done(((bf16[180,320]{1,0:T(8,128)(2,1)}), bf16[180,320]{1,0:T(8,128)(2,1)}) %all-reduce.8.cloned.1.call-update) | async-done | bytes 115216 | tf_op jit(solution)/shard_map/psum | solution.py:107
  600.1 2.0 divide_subtract_fusion
  (62 shorter events, 7.3 us)
Async XLA Ops:
  7.2 14.4 %copy-start.3 = (bf16[1,1,8,128,320]{3,4,2,1,0:T(8,128)(2,1)S(1)}, bf16[1,1,8,128,320]{3,4,2,1,0:T(8,128)(2,1)}, u32[]{:S(2)}) copy-start(bf16[1,1,8,128,320]{3,4,2,1,0:T(8,128)(2,1)} %param.10) | copy-start | bytes 1966084
  7.2 73.9 %all-gather.3.cloned.1.call-start = ((), (), s32[]{:S(2)}) async-start(), calls=%async_computation.1 | async-start | bytes 2402304 | tf_op jit(solution)/shard_map/all_gather | solution.py:72
  8.9 591.2 %all-reduce.8.cloned.1.call-start = ((), (), s32[]{:S(2)}) async-start(), calls=%async_computation | async-start | bytes 282624 | tf_op jit(solution)/shard_map/psum | solution.py:107
  10.9 14.3 %collective-permute-start = (bf16[1,128,320]{1,2,0:T(8,128)(2,1)S(1)}, bf16[1,128,320]{1,2,0:T(8,128)(2,1)S(1)}, u32[]{:S(2)}, u32[]{:S(2)}) collective-permute-start(bf16[1,128,320]{1,2,0:T(8,128)(2,1)S(1)} %get-tuple-element.46), channel_id=1, source_target_pairs={{16,0},{32,16},{48,32},{64,48},{80,64},{96,80},{112,96},{128,112},... | collective-permute-start | bytes 245768 | tf_op jit(solution)/shard_map/ppermute | solution.py:20
  19.7 5.5 collective-permute-start.1
  83.8 140.5 %copy-start.6 = (f32[320]{0:T(512)S(1)}, f32[320]{0:T(512)}, u32[]{:S(2)}) copy-start(f32[320]{0:T(512)} %param.12) | copy-start | bytes 3844
  83.8 140.5 %copy-start.7 = (f32[320]{0:T(512)S(1)}, f32[320]{0:T(512)}, u32[]{:S(2)}) copy-start(f32[320]{0:T(512)} %param.13) | copy-start | bytes 3844
  299.8 149.2 %copy-start = (bf16[16,180,320]{2,1,0:T(8,128)(2,1)S(1)}, bf16[16,180,320]{2,1,0:T(8,128)(2,1)}, u32[]{:S(2)}) copy-start(bf16[16,180,320]{2,1,0:T(8,128)(2,1)} %all-gather.3.cloned.1.call-done) | copy-start | bytes 5529604
  334.1 141.9 %collective-permute-start.4 = (bf16[180,320]{1,0:T(8,128)(2,1)S(1)}, bf16[180,320]{1,0:T(8,128)(2,1)S(1)}, u32[]{:S(2)}, u32[]{:S(2)}) collective-permute-start(bf16[180,320]{1,0:T(8,128)(2,1)S(1)} %slice.98), channel_id=1, source_target_pairs={{0,1},{1,2},{2,3},{3,4},{4,5},{5,6},{6,7},{7,8},{8,9},{9,10},{10,1... | collective-permute-start | bytes 345608
  337.5 120.2 %collective-permute-start.3 = (bf16[1,128,320]{1,2,0:T(8,128)(2,1)}, bf16[1,128,320]{1,2,0:T(8,128)(2,1)S(1)}, u32[]{:S(2)}, u32[]{:S(2)}) collective-permute-start(bf16[1,128,320]{1,2,0:T(8,128)(2,1)} %constant_dynamic-slice_fusion.1), channel_id=1, source_target_pairs={{0,16},{16,32},{32,48},{48,64},{64,80},{80,96},{96,112},{112,128},... | collective-permute-start | bytes 245768 | tf_op jit(solution)/shard_map/ppermute | solution.py:18
  342.6 115.2 %collective-permute-start.2 = (bf16[1,128,320]{1,2,0:T(8,128)(2,1)}, bf16[1,128,320]{1,2,0:T(8,128)(2,1)S(1)}, u32[]{:S(2)}, u32[]{:S(2)}) collective-permute-start(bf16[1,128,320]{1,2,0:T(8,128)(2,1)} %slice_bitcast_fusion), channel_id=1, source_target_pairs={{16,0},{32,16},{48,32},{64,48},{80,64},{96,80},{112,96},{128,112},... | collective-permute-start | bytes 245768 | tf_op jit(solution)/shard_map/ppermute | solution.py:20
  467.5 10.2 %copy-start.1 = (bf16[9,320,320]{2,1,0:T(8,128)(2,1)S(1)}, bf16[9,320,320]{2,1,0:T(8,128)(2,1)}, u32[]{:S(2)}) copy-start(bf16[9,320,320]{2,1,0:T(8,128)(2,1)} %copy.34) | copy-start | bytes 5529604
  482.6 117.5 %copy-start.2 = (f32[180,320]{1,0:T(8,128)S(1)}, f32[180,320]{1,0:T(8,128)}, u32[]{:S(2)}) copy-start(f32[180,320]{1,0:T(8,128)} %param.11) | copy-start | bytes 691204
  482.7 117.4 %copy-start.4 = (f32[180,320]{1,0:T(8,128)S(1)}, f32[180,320]{1,0:T(8,128)}, u32[]{:S(2)}) copy-start(f32[180,320]{1,0:T(8,128)} %param.14) | copy-start | bytes 691204
  482.7 117.4 %copy-start.5 = (f32[180,320]{1,0:T(8,128)S(1)}, f32[180,320]{1,0:T(8,128)}, u32[]{:S(2)}) copy-start(f32[180,320]{1,0:T(8,128)} %param.15) | copy-start | bytes 691204
Sparse Core Ops, SparseCore 0:
  10.7 70.3 all-gather.2
  477.8 122.2 all-reduce.7
where the time goes:
time: 610 us; the launch traced here: 609 us
  blocking collectives  331 us (54%)
  waiting for transfers between devices  154 us (25%)
  local copies, waits for them, and re-layouts  55.7 us (9%)
  starting transfers between devices  23.8 us (4%)
  matrix products  17.4 us (3%)
  between operations  15.7 us (3%)
  other arithmetic  11.1 us (2%)
    psum x1, waiting for transfers between devices, local(): lax.psum(lax.dot_general(columns, pre_grad, (((0,), (0,)), ((), ())), pre...  116 us
    psum x1, blocking collectives, local(): lax.psum((jnp.sum(dshift * normed, axis=0), jnp.sum(dshift, axis=0)), ('t...  101 us
    psum x1, blocking collectives, local(): group_mean = lax.psum(grouped(mixed * cell_mask), 'tile') / population  71.5 us
    psum x1, blocking collectives, local(): lax.psum((grouped(scaled), grouped(scaled * normed)), 'tile')  62.9 us
    psum x1, blocking collectives, local(): variance = lax.psum(grouped(centered * centered), 'tile') / population  62.7 us
    all_gather x1, waiting for transfers between devices, local(): lax.all_gather(master_weight.astype(jnp.bfloat16), 'fsdp', axis=0, tiled=...  37.7 us
    unnamed x1, blocking collectives  33.6 us
    unnamed x41, local copies, waits for them, and re-layouts  25.8 us
  transfers between devices with their start and end apart: 7, of which 2 were waited for; matrix products, arithmetic and copies ran while one was open for 9% of the time, Pallas kernels for 0%

commit v1 on v0

--- a/solution.py
+++ b/solution.py
@@ -5,6 +5,16 @@
 
 GROUPS = 32
 ROWS_MEAN = 5
+
+
+def test_group(piece_in, axis_key, at_axis):
+    inbox = []
+    for _ in range(jax.lax.psum(1, axis_name=axis_key)):
+        inbox.append(piece_in)
+    return jnp.concatenate(
+        jax.lax.all_to_all(jnp.stack(inbox), split_axis=0, axis_name=axis_key, concat_axis=0),
+        at_axis,
+    )
 
 
 def extended(cells, sides, width):
@@ -69,7 +79,7 @@
     source = jnp.where(live_rows[:, None, None], images[0, 0], jnp.zeros((), jnp.bfloat16))
     beside_all = extended(edge_pair(source, live_count), (("tile", 0),), 1)
     columns = patches_of(framed(source, beside_all, live_count), slot_count, cell_cols)
-    gathered = lax.all_gather(master_weight.astype(jnp.bfloat16), "fsdp", axis=0, tiled=True)
+    gathered = test_group(master_weight.astype(jnp.bfloat16), axis_key="fsdp", at_axis=0)
     mixed = jnp.dot(columns, gathered, preferred_element_type=jnp.float32)
     group_mean = lax.psum(grouped(mixed * cell_mask), "tile") / population
     centered = (mixed - spread(group_mean)) * cell_mask

time: 610 us -> 658 us (1.079)
  waiting for transfers between devices: 154 us -> 186 us
  starting transfers between devices: 23.8 us -> 34.2 us
    all_to_all x0 -> x1, waiting for transfers between devices: none -> 68.2 us  [test_group(): jax.lax.all_to_all(jnp.stack(inbox), split_axis=0, axis_name=axis_key, co...]
    all_gather x1 -> x0, waiting for transfers between devices: 37.7 us -> none  [local(): lax.all_gather(master_weight.astype(jnp.bfloat16), 'fsdp', axis=0, tiled=...]
    all_to_all x0 -> x1, starting transfers between devices: none -> 15.7 us  [test_group(): jax.lax.all_to_all(jnp.stack(inbox), split_axis=0, axis_name=axis_key, co...]
    unnamed x41 -> x36, local copies, waits for them, and re-layouts: 25.8 us -> 23 us
where the time goes in v1:
time: 658 us; the launch traced here: 657 us
  blocking collectives  330 us (50%)
  waiting for transfers between devices  186 us (28%)
  local copies, waits for them, and re-layouts  57.9 us (9%)
  starting transfers between devices  34.2 us (5%)
  matrix products  19.2 us (3%)
  between operations  15.6 us (2%)
  other arithmetic  14 us (2%)
    psum x1, waiting for transfers between devices, local(): lax.psum(lax.dot_general(columns, pre_grad, (((0,), (0,)), ((), ())), pre...  117 us
    psum x1, blocking collectives, local(): lax.psum((jnp.sum(dshift * normed, axis=0), jnp.sum(dshift, axis=0)), ('t...  101 us
    all_to_all x1, waiting for transfers between devices, test_group(): jax.lax.all_to_all(jnp.stack(inbox), split_axis=0, axis_name=axis_key, co...  68.2 us
    psum x1, blocking collectives, local(): group_mean = lax.psum(grouped(mixed * cell_mask), 'tile') / population  67.1 us
    psum x1, blocking collectives, local(): variance = lax.psum(grouped(centered * centered), 'tile') / population  62.9 us
    psum x1, blocking collectives, local(): lax.psum((grouped(scaled), grouped(scaled * normed)), 'tile')  62.9 us
    unnamed x1, blocking collectives  36 us
    unnamed x36, local copies, waits for them, and re-layouts  23 us
  transfers between devices with their start and end apart: 7, of which 2 were waited for; matrix products, arithmetic and copies ran while one was open for 9% of the time, Pallas kernels for 0%

profile of v1, /device:TPU:1, one launch (start us, length us, event | category | flops | bytes accessed | tf_op | source)
XLA Modules:
  0.0 656.9 jit_solution(14443801103932754480)
XLA Ops:
  7.2 1.0 convert_element_type.38
  8.1 1.7 stack.2
  9.8 15.7 %all-to-all-start = ((bf16[16,180,320]{2,1,0:T(8,128)(2,1)}), bf16[16,180,320]{2,1,0:T(8,128)(2,1)S(1)}, u32[]{:S(2)}, u32[]{:S(2)}) async-start(bf16[16,180,320]{2,1,0:T(8,128)(2,1)} %stack.2), calls=%async_computation | async-start | bytes 4521984 | tf_op jit(solution)/shard_map/all_to_all | solution.py:15
  26.3 1.2 bitcast_select_fusion
  27.5 2.9 collective-permute-start
  30.4 3.0 collective-permute-start.1
  33.4 2.5 copy.30
  36.0 1.3 dynamic-slice.4
  38.2 1.1 fusion.5
  39.3 1.0 slice_dynamic-update-slice_fusion.5
  40.4 1.1 fusion.6
  41.5 1.1 fusion.7
  42.6 1.0 slice_dynamic-update-slice_fusion.4
  43.6 1.1 fusion.8
  44.6 1.1 fusion.9
  46.7 1.1 fusion.10
  47.8 8.4 %copy.29 = bf16[8,128,2880]{2,1,0:T(8,128)(2,1)} copy(bf16[8,128,2880]{1,2,0:T(8,128)(2,1)} %fusion.10) | data formatting | bytes 11796480 | tf_op jit(solution)/shard_map/concatenate | solution.py:58
  56.2 68.2 %all-to-all-done = bf16[16,180,320]{2,1,0:T(8,128)(2,1)S(1)} async-done(((bf16[16,180,320]{2,1,0:T(8,128)(2,1)}), bf16[16,180,320]{2,1,0:T(8,128)(2,1)S(1)}, u32[]{:S(2)}, u32[]{:S(2)}) %all-to-all-start) | async-done | bytes 1843232 | tf_op jit(solution)/shard_map/all_to_all | solution.py:15
  124.4 2.2 reshape.72
  126.7 6.8 %multiply_reduce_fusion.3 = (f32[320]{0:T(512)S(1)}, f32[1024,320]{0,1:T(8,128)}) fusion(f32[1024]{0:T(1024)S(1)} %broadcast_bitcast_fusion, bf16[1024,2880]{1,0:T(8,128)(2,1)} %bitcast.57, bf16[2880,320]{1,0:T(8,128)(2,1)} %reshape.72), kind=kOutput, calls=%fused_computation.26 | convolution fusion | flops 1888091904 | bytes 9057536 | tf_op jit(solution)/shard_map/dot_general | solution.py:83
  133.7 67.1 %psum.49 = f32[32]{0:T(128)S(1)} all-reduce(f32[32]{0:T(128)S(1)} %reduce_sum.67), channel_id=1, replica_groups=mesh['tile'=32,'fsdp'=16] {'tile'}, use_global_device_ids=true, to_apply=%region_2.3 | all-reduce | flops 32 | bytes 256 | tf_op jit(solution)/shard_map/psum | solution.py:84
  201.0 1.7 multiply_reduce_fusion.2
  202.9 62.9 %psum.50 = f32[32]{0:T(128)S(1)} all-reduce(f32[32]{0:T(128)S(1)} %reduce_sum.73), channel_id=1, replica_groups=mesh['tile'=32,'fsdp'=16] {'tile'}, use_global_device_ids=true, to_apply=%region_5.6 | all-reduce | flops 32 | bytes 256 | tf_op jit(solution)/shard_map/psum | solution.py:86
  266.0 4.2 multiply_reduce_fusion
  270.6 62.9 %all-reduce.5 = (f32[32]{0:T(128)S(1)}, f32[32]{0:T(128)S(1)}) all-reduce(f32[32]{0:T(128)S(1)} %reduce_sum.93, f32[32]{0:T(128)S(1)} %reduce_sum.90), channel_id=1, replica_groups=mesh['tile'=32,'fsdp'=16] {'tile'}, use_global_device_ids=true, to_apply=%region_11.12 | all-reduce | flops 64 | bytes 512 | tf_op jit(solution)/shard_map/psum | solution.py:95
  333.8 2.5 multiply_convert_fusion
  336.4 7.4 %convolution_convert_fusion = bf16[2880,320]{1,0:T(8,128)(2,1)} fusion(bf16[1024,2880]{1,0:T(8,128)(2,1)} %bitcast.58, bf16[1024,320]{0,1:T(8,128)(2,1)S(1)} %multiply_convert_fusion), kind=kOutput, calls=%fused_computation | convolution fusion | flops 1888358400 | bytes 8396800 | tf_op jit(solution)/shard_map/dot_general | solution.py:118
  344.6 36.0 %fusion = bf16[192,320]{1,0:T(8,128)(2,1)S(1)} fusion(bf16[2880,320]{1,0:T(8,128)(2,1)} %convolution_convert_fusion), kind=kCustom, calls=%all-reduce-scatter | all-reduce-scatter fusion | flops 983041 | bytes 1968128
  380.6 2.0 collective-permute-start.4
  383.3 5.3 collective-permute-start.3
  388.6 5.2 collective-permute-start.2
  393.8 101.4 %all-reduce.4 = (f32[320]{0:T(512)S(1)}, f32[320]{0:T(512)S(1)}) all-reduce(f32[320]{0:T(512)S(1)} %get-tuple-element.32, f32[320]{0:T(512)S(1)} %get-tuple-element.35), channel_id=1, replica_groups=mesh['tile'=32,'fsdp'=16] {'tile','fsdp'}, use_global_device_ids=true, to_apply=%region_15.16 | all-reduce | flops 640 | bytes 5120 | tf_op jit(solution)/shard_map/psum | solution.py:96
  495.8 2.2 reshape_reshape.3
  498.0 1.8 reverse_bitcast_fusion
  499.8 2.5 copy.34
  502.3 1.2 copy.38
  504.7 1.1 fusion.11
  505.8 1.0 slice_dynamic-update-slice_fusion.2
  506.8 1.1 fusion.12
  507.9 1.1 fusion.13
  509.0 1.0 slice_dynamic-update-slice_fusion.1
  510.0 1.1 fusion.14
  511.1 1.1 fusion.15
  513.2 1.1 fusion.16
  514.2 8.6 %copy.33 = bf16[8,128,2880]{2,1,0:T(8,128)(2,1)} copy(bf16[8,128,2880]{1,2,0:T(8,128)(2,1)} %fusion.16) | data formatting | bytes 11796480 | tf_op jit(solution)/shard_map/concatenate | solution.py:58
  524.5 5.0 fusion.4
  530.5 117.5 %all-reduce.8.cloned.1.call-done = bf16[180,320]{1,0:T(8,128)(2,1)} async-done(((bf16[180,320]{1,0:T(8,128)(2,1)}), bf16[180,320]{1,0:T(8,128)(2,1)}) %all-reduce.8.cloned.1.call-update) | async-done | bytes 115216 | tf_op jit(solution)/shard_map/psum | solution.py:117
  648.0 2.0 divide_subtract_fusion
  (58 shorter events, 9.8 us)
Async XLA Ops:
  9.8 114.6 %all-to-all-start = ((bf16[16,180,320]{2,1,0:T(8,128)(2,1)}), bf16[16,180,320]{2,1,0:T(8,128)(2,1)S(1)}, u32[]{:S(2)}, u32[]{:S(2)}) async-start(bf16[16,180,320]{2,1,0:T(8,128)(2,1)} %stack.2), calls=%async_computation | async-start | bytes 4521984 | tf_op jit(solution)/shard_map/all_to_all | solution.py:15
  25.6 622.4 %all-reduce.8.cloned.1.call-start = ((), (), s32[]{:S(2)}) async-start(), calls=%async_computation.1 | async-start | bytes 282624 | tf_op jit(solution)/shard_map/psum | solution.py:117
  27.5 10.5 %collective-permute-start = (bf16[1,128,320]{1,2,0:T(8,128)(2,1)S(1)}, bf16[1,128,320]{1,2,0:T(8,128)(2,1)S(1)}, u32[]{:S(2)}, u32[]{:S(2)}) collective-permute-start(bf16[1,128,320]{1,2,0:T(8,128)(2,1)S(1)} %get-tuple-element.46), channel_id=1, source_target_pairs={{16,0},{32,16},{48,32},{64,48},{80,64},{96,80},{112,96},{128,112},... | collective-permute-start | bytes 245768 | tf_op jit(solution)/shard_map/ppermute | solution.py:30
  30.4 7.7 %collective-permute-start.1 = (bf16[1,128,320]{1,2,0:T(8,128)(2,1)S(1)}, bf16[1,128,320]{1,2,0:T(8,128)(2,1)S(1)}, u32[]{:S(2)}, u32[]{:S(2)}) collective-permute-start(bf16[1,128,320]{1,2,0:T(8,128)(2,1)S(1)} %get-tuple-element.47), channel_id=1, source_target_pairs={{0,16},{16,32},{32,48},{48,64},{64,80},{80,96},{96,112},{112,128},... | collective-permute-start | bytes 245768 | tf_op jit(solution)/shard_map/ppermute | solution.py:28
  126.7 139.3 %copy-start.4 = (f32[320]{0:T(512)S(1)}, f32[320]{0:T(512)}, u32[]{:S(2)}) copy-start(f32[320]{0:T(512)} %param.12) | copy-start | bytes 3844
  126.7 139.3 %copy-start.5 = (f32[320]{0:T(512)S(1)}, f32[320]{0:T(512)}, u32[]{:S(2)}) copy-start(f32[320]{0:T(512)} %param.13) | copy-start | bytes 3844
  380.6 142.2 %collective-permute-start.4 = (bf16[180,320]{1,0:T(8,128)(2,1)S(1)}, bf16[180,320]{1,0:T(8,128)(2,1)S(1)}, u32[]{:S(2)}, u32[]{:S(2)}) collective-permute-start(bf16[180,320]{1,0:T(8,128)(2,1)S(1)} %slice.98), channel_id=1, source_target_pairs={{0,1},{1,2},{2,3},{3,4},{4,5},{5,6},{6,7},{7,8},{8,9},{9,10},{10,1... | collective-permute-start | bytes 345608
  383.3 121.2 %collective-permute-start.3 = (bf16[1,128,320]{1,2,0:T(8,128)(2,1)}, bf16[1,128,320]{1,2,0:T(8,128)(2,1)S(1)}, u32[]{:S(2)}, u32[]{:S(2)}) collective-permute-start(bf16[1,128,320]{1,2,0:T(8,128)(2,1)} %constant_dynamic-slice_fusion.1), channel_id=1, source_target_pairs={{0,16},{16,32},{32,48},{48,64},{64,80},{80,96},{96,112},{112,128},... | collective-permute-start | bytes 245768 | tf_op jit(solution)/shard_map/ppermute | solution.py:28
  388.6 115.9 %collective-permute-start.2 = (bf16[1,128,320]{1,2,0:T(8,128)(2,1)}, bf16[1,128,320]{1,2,0:T(8,128)(2,1)S(1)}, u32[]{:S(2)}, u32[]{:S(2)}) collective-permute-start(bf16[1,128,320]{1,2,0:T(8,128)(2,1)} %slice_bitcast_fusion), channel_id=1, source_target_pairs={{16,0},{32,16},{48,32},{64,48},{80,64},{96,80},{112,96},{128,112},... | collective-permute-start | bytes 245768 | tf_op jit(solution)/shard_map/ppermute | solution.py:30
  514.2 10.2 %copy-start = (bf16[9,320,320]{2,1,0:T(8,128)(2,1)S(1)}, bf16[9,320,320]{2,1,0:T(8,128)(2,1)}, u32[]{:S(2)}) copy-start(bf16[9,320,320]{2,1,0:T(8,128)(2,1)} %copy.34) | copy-start | bytes 5529604
  529.4 118.6 %copy-start.1 = (f32[180,320]{1,0:T(8,128)S(1)}, f32[180,320]{1,0:T(8,128)}, u32[]{:S(2)}) copy-start(f32[180,320]{1,0:T(8,128)} %param.11) | copy-start | bytes 691204
  529.4 118.6 %copy-start.2 = (f32[180,320]{1,0:T(8,128)S(1)}, f32[180,320]{1,0:T(8,128)}, u32[]{:S(2)}) copy-start(f32[180,320]{1,0:T(8,128)} %param.14) | copy-start | bytes 691204
  529.4 118.5 %copy-start.3 = (f32[180,320]{1,0:T(8,128)S(1)}, f32[180,320]{1,0:T(8,128)}, u32[]{:S(2)}) copy-start(f32[180,320]{1,0:T(8,128)} %param.15) | copy-start | bytes 691204
Sparse Core Ops, SparseCore 0:
  524.6 123.3 all-reduce.7
